TPU v7x, 256 devices: a whole 4x4x8 slice. The times are simulated.
256 devices in a mesh: ang: 128 (over x_lo, z, y, core), row: 2 (over x_hi).
Axes of the slice: x: 4 (x_hi: 2, x_lo: 2; x = x_hi * 2 + x_lo), y: 4, z: 8, core: 2. Of those that a mesh axis runs over, the one named last changes fastest.
Arguments:
- sample: bfloat16 [256, 20, 256, 128], P('ang', None, 'row')
- flat_speckle: bfloat16 [20, 256, 128], P(None, 'row')
- peak_shift: int32 [2, 256, 256, 128], P(None, 'ang', 'row'), may hold values from -2 to 2, as said below
- partner: int32 [256], P('ang'), may hold values from 0 to 255, as said below
Outputs:
- sinogram: float32 [2, 256, 256, 128], P(None, ('row', 'ang'))
Inputs may be any that keep to these rules, and one draw needn't show every extreme that they name: partner[j] lies in the block of 2 projections that starts at ((j // 2 + 256 // 4) % 128) * 2, and partner[partner[j]] = j. peak_shift is the same on every pixel of an aligned tile of 4 x 4 pixels of one projection.
All inputs are finite; a program needn't handle non-finite values.
Results may differ from a plain program's by a relative error of at most 0.0003.
Values may be sent and summed in bfloat16 or wider, within the bound.
No kernel may reach another device: no remote copies, remote signals or barrier semaphores. Data moves between devices by JAX's collectives and lax.ppermute only.
A program may use at most 320 MiB of HBM per device.

v0:
```python
import jax
import jax.numpy as jnp
from jax import lax
from jax.sharding import PartitionSpec as P

EDGE = 128
CYCLE = 8


SHARPNESS = 12.0
EPSILON = 1e-05


def shifted(block, axis, distance):
    devices = range(lax.axis_size(axis))
    route = [((i - distance) % len(devices), i) for i in devices]
    return lax.ppermute(block, axis, route)


def padded_2(block, sides, width):
    for axis, dim in sides:
        count = lax.axis_size(axis)
        forward = [(i, i + 1) for i in range(count - 1)]
        backward = [(target, source) for source, target in forward]
        low = lax.ppermute(
            lax.slice_in_dim(block, block.shape[dim] - width, None, axis=dim), axis, forward
        )
        high = lax.ppermute(lax.slice_in_dim(block, 0, width, axis=dim), axis, backward)
        block = jnp.concatenate([low, block, high], axis=dim)
    return block


def window_sum(values, axis):
    length = values.shape[axis] - 6
    total = lax.slice_in_dim(values, 0, length, axis=axis)
    for offset in range(1, 7):
        total = total + lax.slice_in_dim(values, offset, offset + length, axis=axis)
    return total


def box_window(values):
    return window_sum(window_sum(values, values.ndim - 2), values.ndim - 1)


def stitch(own_edge, far_edge):
    edge_cols = own_edge.shape[-1]
    position = jnp.arange(edge_cols).astype(jnp.float32)
    own_weight = (edge_cols - 0.5 - position) / edge_cols
    far_weight = (position + 0.5) / edge_cols
    blended = own_weight * own_edge.astype(jnp.float32) + far_weight * far_edge.astype(jnp.float32)
    return blended.astype(jnp.bfloat16)


def track(padded, flat_pad, energy_ref, shift_rows, shift_cols):
    rows = padded.shape[-2] - 6
    cols = padded.shape[-1] - 6
    squares = jnp.einsum("pcik,pcik->pik", padded, padded, preferred_element_type=jnp.float32)
    energy = box_window(squares)
    total = jnp.zeros(energy.shape, jnp.float32)
    along_rows = jnp.zeros(energy.shape, jnp.float32)
    along_cols = jnp.zeros(energy.shape, jnp.float32)
    for row_shift in range(-3, 4):
        for col_shift in range(-3, 4):
            moved = lax.slice(
                flat_pad,
                (0, 3 + row_shift, 3 + col_shift),
                (flat_pad.shape[0], 3 + row_shift + rows + 6, 3 + col_shift + cols + 6),
            )
            product = jnp.einsum("pcik,cik->pik", padded, moved, preferred_element_type=jnp.float32)
            window = box_window(product)
            energy_moved = lax.slice(
                energy_ref,
                (3 + row_shift, 3 + col_shift),
                (3 + row_shift + rows, 3 + col_shift + cols),
            )
            score = window / jnp.sqrt((energy + EPSILON) * (energy_moved + EPSILON))
            off_rows = row_shift - shift_rows
            off_cols = col_shift - shift_cols
            inside = (jnp.abs(off_rows) <= 1) & (jnp.abs(off_cols) <= 1)
            weight = jnp.where(
                inside, jnp.exp(SHARPNESS * score), jnp.zeros(score.shape, score.dtype)
            )
            total = total + weight
            along_rows = along_rows + weight * off_rows.astype(jnp.float32)
            along_cols = along_cols + weight * off_cols.astype(jnp.float32)
    grad_rows = shift_rows.astype(jnp.float32) + along_rows / total
    grad_cols = shift_cols.astype(jnp.float32) + along_cols / total
    return (grad_rows, grad_cols)


def smooth_columns(column_mean, half_width):
    cols = column_mean.shape[-1]
    padded_mean = jnp.pad(column_mean, ((0, 0), (0, 0), (0, 0), (half_width, half_width)))
    summed = lax.slice_in_dim(padded_mean, 0, cols, axis=3)
    for offset in range(1, 2 * half_width + 1):
        summed = summed + lax.slice_in_dim(padded_mean, offset, offset + cols, axis=3)
    position = jnp.arange(cols)
    counted = (
        jnp.minimum(position + half_width, cols - 1) - jnp.maximum(position - half_width, 0) + 1
    ).astype(jnp.float32)
    return summed / counted


def apply_cycles(sinogram, column_mean):
    return sinogram - (column_mean - smooth_columns(column_mean, CYCLE))


def body(sample, flat_speckle, peak_shift, partner):
    angle_count = lax.axis_size("ang")
    count, channels, rows, cols = sample.shape
    arrived = shifted(sample, "ang", angle_count // 2)
    mate_edge = jnp.flip(jnp.take(arrived, partner % count, axis=0), 3)
    seam = stitch(sample, mate_edge)
    stitched = jnp.concatenate([sample[:, :, :, : cols - EDGE], seam], axis=3)
    extended = padded_2(stitched, (("row", 2),), 3)
    padded = jnp.pad(extended, ((0, 0), (0, 0), (0, 0), (3, 3)), mode="reflect")
    flat_rows = padded_2(flat_speckle, (("row", 1),), 6)
    flat_pad = jnp.pad(flat_rows, ((0, 0), (0, 0), (6, 6)), mode="reflect")
    flat_squares = jnp.einsum("cik,cik->ik", flat_pad, flat_pad, preferred_element_type=jnp.float32)
    energy_ref = box_window(flat_squares)
    grad_rows, grad_cols = track(padded, flat_pad, energy_ref, peak_shift[0], peak_shift[1])
    ordered = jnp.transpose(jnp.stack([grad_rows, grad_cols]), (0, 2, 1, 3))
    projections = count * angle_count
    sinogram = lax.all_to_all(ordered, "ang", split_axis=1, concat_axis=2, tiled=True)
    column_mean = jnp.sum(sinogram, axis=2, keepdims=True) / projections
    sinogram = apply_cycles(sinogram, column_mean)
    return sinogram


def solution(mesh):
    in_specs = (
        P("ang", None, "row", None),
        P(None, "row", None),
        P(None, "ang", "row", None),
        P("ang"),
    )
    out_specs = P(None, ("row", "ang"), None, None)
    return jax.shard_map(body, mesh=mesh, in_specs=in_specs, out_specs=out_specs, check_vma=False)
```

profile of v0, /device:TPU:1, one launch (start us, length us, event | category | flops | bytes accessed | tf_op | source)
XLA Modules:
  0.0 320.9 jit_solution(6359179385013286395)
XLA Ops:
  0.8 5.5 %collective-permute-start = (bf16[20,6,128]{2,1,0:T(8,128)(2,1)S(1)}, bf16[20,6,128]{2,1,0:T(8,128)(2,1)S(1)}, u32[]{:S(2)}, u32[]{:S(2)}) collective-permute-start(bf16[20,6,128]{2,1,0:T(8,128)(2,1)S(1)} %get-tuple-element.166), channel_id=1, source_target_pairs={{0,1},{2,3},{4,5},{6,7},{8,9},{10,11},{12,13},{14,15},{16,17},{18,... | collective-permute-start | bytes 92168 | tf_op jit(solution)/shard_map/ppermute | solution.py:25
  6.3 1.3 collective-permute-start.1
  8.7 2.2 abs_compare_fusion
  10.9 1.7 collective-permute-done.1
  12.5 1.3 pad_maximum_fusion.4
  14.3 4.2 %rev.22 = bf16[20,140,6]{2,1,0:T(8,128)(2,1)S(1)} reverse(bf16[20,140,6]{2,1,0:T(8,128)(2,1)S(1)} %get-tuple-element.164), dimensions={2} | reverse | bytes 67200 | tf_op jit(solution)/shard_map/jit(_pad)/jit(_flip)/rev | solution.py:118
  18.5 4.2 %rev.26 = bf16[20,140,6]{2,1,0:T(8,128)(2,1)S(1)} reverse(bf16[20,140,6]{2,1,0:T(8,128)(2,1)S(1)} %get-tuple-element.165), dimensions={2} | reverse | bytes 67200 | tf_op jit(solution)/shard_map/jit(_pad)/jit(_flip)/rev | solution.py:118
  22.7 1.4 fusion.50
  24.0 15.9 %fusion.83 = (f32[134,134,20]{1,0,2:T(8,128)}, f32[134,134,20]{1,0,2:T(8,128)}, f32[134,134,20]{1,0,2:T(8,128)}, f32[134,134,20]{1,0,2:T(8,128)}, f32[134,134,20...) fusion(bf16[20,140,140]{2,1,0:T(8,128)(2,1)S(1)} %get-tuple-ele, ...), kind=kLoop, calls=%fused_computation.173 | loop fusion | flops 5745920 | bytes 34475520
  40.0 18.9 %fusion.84 = (f32[134,134,20]{1,0,2:T(8,128)}, f32[134,134,20]{1,0,2:T(8,128)}, f32[134,134,20]{1,0,2:T(8,128)}, f32[134,134,20]{1,0,2:T(8,128)}, f32[134,134,20...) fusion(bf16[20,140,140]{2,1,0:T(8,128)(2,1)S(1)} %get-tuple-ele, ...), kind=kLoop, calls=%fused_computation.175 | loop fusion | flops 6823280 | bytes 40939680
  59.3 1.3 slice_add_fusion.612
  60.7 2.0 pad_maximum_fusion.2
  62.7 1.3 slice_add_fusion.631
  64.0 12.8 %fusion.78 = (f32[134,134,20]{1,0,2:T(8,128)}, f32[134,134,20]{1,0,2:T(8,128)}, f32[134,134,20]{1,0,2:T(8,128)}, f32[134,134,20]{1,0,2:T(8,128)}, f32[134,134,20...) fusion(bf16[20,140,134]{2,1,0:T(8,128)(2,1)S(1)} %get-tuple-ele, ...), kind=kLoop, calls=%fused_computation.163 | loop fusion | flops 5027680 | bytes 30166080
  76.8 2.1 gather_fusion
  79.1 3.8 %rev.23 = bf16[2,20,128,128]{3,2,1,0:T(8,128)(2,1)S(1)} reverse(bf16[2,20,128,128]{3,2,1,0:T(8,128)(2,1)S(1)} %broadcast_select_fusion), dimensions={3} | reverse | bytes 2621440 | tf_op jit(solution)/shard_map/jit(_flip)/rev | solution.py:112
  82.9 1.8 add_convert_fusion
  84.8 4.4 %collective-permute-start.3 = (bf16[2,20,3,128]{3,2,1,0:T(4,128)(2,1)S(1)}, bf16[2,20,3,128]{3,2,1,0:T(4,128)(2,1)S(1)}, u32[]{:S(2)}, u32[]{:S(2)}) collective-permute-start(bf16[2,20,3,128]{3,2,1,0:T(4,128)(2,1)S(1)} %get-tuple-element.160), channel_id=1, source_target_pairs={{0,1},{2,3},{4,5},{6,7},{8,9},{10,11},{12,13},{14,15},{16,17},{18,... | collective-permute-start | bytes 92168 | tf_op jit(solution)/shard_map/ppermute | solution.py:25
  89.2 1.5 collective-permute-start.4
  91.8 3.6 %collective-permute-done.4 = bf16[2,20,3,128]{3,2,1,0:T(4,128)(2,1)S(1)} collective-permute-done((bf16[2,20,3,128]{3,2,1,0:T(4,128)(2,1)S(1)}, bf16[2,20,3,128]{3,2,1,0:T(4,128)(2,1)S(1)}, u32[]{:S(2)}, u32[]{:S(2)}) %collective-permute-start.4) | collective-permute-done | bytes 30752 | tf_op jit(solution)/shard_map/ppermute | solution.py:28
  96.8 27.6 %rev.24 = bf16[2,20,134,3]{3,2,1,0:T(8,128)(2,1)} reverse(bf16[2,20,134,3]{3,2,1,0:T(8,128)(2,1)S(1)} %get-tuple-element.158), dimensions={3} | reverse | bytes 64320 | tf_op jit(solution)/shard_map/jit(_pad)/jit(_flip)/rev | solution.py:116
  124.5 27.6 %rev.25 = bf16[2,20,134,3]{3,2,1,0:T(8,128)(2,1)} reverse(bf16[2,20,134,3]{3,2,1,0:T(8,128)(2,1)S(1)} %get-tuple-element.159), dimensions={3} | reverse | bytes 64320 | tf_op jit(solution)/shard_map/jit(_pad)/jit(_flip)/rev | solution.py:116
  152.1 15.9 %fusion.2 = (f32[134,134,2]{1,0,2:T(8,128)}, f32[134,134,2]{1,0,2:T(8,128)}, f32[134,134,2]{1,0,2:T(8,128)}, f32[134,134,2]{1,0,2:T(8,128)}, f32[134,134,2]{1,0,...) fusion(f32[134,134,20]{1,0,2:T(8,128)} %get-tuple-element.141, ...), kind=kLoop, calls=%fused_computation.52 | loop fusion | flops 26108024 | bytes 23414624 | tf_op jit(solution)/shard_map/pcik,cik->pik/dot_general | solution.py:69
  168.0 1.4 fusion.49
  169.3 19.1 %fusion = (f32[134,134,2]{1,0,2:T(8,128)S(1)}, f32[134,134,2]{1,0,2:T(8,128)}, f32[134,134,2]{1,0,2:T(8,128)}, f32[134,134,2]{1,0,2:T(8,128)}, f32[134,134,2]{1,...) fusion(f32[134,134,20]{1,0,2:T(8,128)} %get-tuple-element.157, ...), kind=kLoop, calls=%fused_computation.50 | loop fusion | flops 25928464 | bytes 29878784 | tf_op jit(solution)/shard_map/pcik,cik->pik/dot_general | solution.py:69
  188.5 2.8 slice_add_fusion.102
  206.0 19.4 %fusion.1 = (f32[134,134,2]{1,0,2:T(8,128)}, f32[134,134,2]{1,0,2:T(8,128)}, f32[134,134,2]{1,0,2:T(8,128)}, f32[134,134,2]{1,0,2:T(8,128)}, f32[134,134,2]{1,0,...) fusion(f32[134,134,20]{1,0,2:T(8,128)} %get-tuple-element.142, ...), kind=kLoop, calls=%fused_computation.51 | loop fusion | flops 25928464 | bytes 29878784 | tf_op jit(solution)/shard_map/pcik,cik->pik/dot_general | solution.py:69
  225.3 2.4 slice_add_fusion
  250.2 34.3 %fusion.391 = (f32[1,2,128,128]{3,2,1,0:T(8,128)}, f32[2,128,128]{2,1,0:T(8,128)S(1)}, f32[2,128,128]{2,1,0:T(8,128)}, f32[2,128,128]{2,1,0:T(8,128)}, f32[2,128...) fusion(s32[2,2,128,128]{3,2,1,0:T(8,128)} %param.6, ...), kind=kLoop, calls=%fused_computation.1223 | loop fusion | flops 22806528 | bytes 56229888 | tf_op jit(solution)/shard_map/stack | solution.py:122
  284.5 3.9 %fusion.346 = f32[1,2,128,128]{3,2,1,0:T(8,128)S(1)} fusion(f32[2,128,128]{2,1,0:T(8,128)} %get-tuple-element.103, f32[2,128,128]{2,1,0:T(8,128)} %get-tuple-element.102, f32[2,128,128]{2,1,0:T(8,128)} %get-tuple-element.101, f32[2,128,128]{2,1,0:T(8,128)} %get-tuple-element.100, f32[2,128,128]{2,1,0:T(8,128)} %get-tuple-element.99, ...), kind=kLoop, calls=%fused_computation.1119 | loop fusion | flops 5308416 | bytes 6684672 | tf_op jit(solution)/shard_map/stack | solution.py:122
  289.3 15.4 %all-to-all-start = ((f32[2,128,2,128]{3,2,0,1:T(2,128)}), f32[2,128,2,128]{3,2,0,1:T(2,128)S(1)}, u32[]{:S(2)}, u32[]{:S(2)}) async-start(f32[2,128,2,128]{3,2,0,1:T(2,128)} %copy.14), calls=%async_computation | async-start | bytes 524288 | tf_op jit(solution)/shard_map/all_to_all | solution.py:124
  304.7 15.1 %all-to-all-done = f32[2,128,2,128]{3,2,0,1:T(2,128)S(1)} async-done(((f32[2,128,2,128]{3,2,0,1:T(2,128)}), f32[2,128,2,128]{3,2,0,1:T(2,128)S(1)}, u32[]{:S(2)}, u32[]{:S(2)}) %all-to-all-start) | async-done | bytes 262176 | tf_op jit(solution)/shard_map/all_to_all | solution.py:124
  (218 shorter events, 44.3 us)
Async XLA Ops:
  0.8 10.0 %collective-permute-start = (bf16[20,6,128]{2,1,0:T(8,128)(2,1)S(1)}, bf16[20,6,128]{2,1,0:T(8,128)(2,1)S(1)}, u32[]{:S(2)}, u32[]{:S(2)}) collective-permute-start(bf16[20,6,128]{2,1,0:T(8,128)(2,1)S(1)} %get-tuple-element.166), channel_id=1, source_target_pairs={{0,1},{2,3},{4,5},{6,7},{8,9},{10,11},{12,13},{14,15},{16,17},{18,... | collective-permute-start | bytes 92168 | tf_op jit(solution)/shard_map/ppermute | solution.py:25
  6.3 6.3 %collective-permute-start.1 = (bf16[20,6,128]{2,1,0:T(8,128)(2,1)S(1)}, bf16[20,6,128]{2,1,0:T(8,128)(2,1)S(1)}, u32[]{:S(2)}, u32[]{:S(2)}) collective-permute-start(bf16[20,6,128]{2,1,0:T(8,128)(2,1)S(1)} %get-tuple-element.167), channel_id=1, source_target_pairs={{1,0},{3,2},{5,4},{7,6},{9,8},{11,10},{13,12},{15,14},{17,16},{19,... | collective-permute-start | bytes 92168 | tf_op jit(solution)/shard_map/ppermute | solution.py:28
  7.6 69.2 %collective-permute-start.2 = (bf16[2,20,128,128]{3,2,1,0:T(8,128)(2,1)}, bf16[2,20,128,128]{3,2,1,0:T(8,128)(2,1)}, u32[]{:S(2)}, u32[]{:S(2)}) collective-permute-start(bf16[2,20,128,128]{3,2,1,0:T(8,128)(2,1)} %param.4), channel_id=1, source_target_pairs={{128,0},{130,2},{132,4},{134,6},{136,8},{138,10},{140,12},{142,14}... | collective-permute-start | bytes 3932168 | tf_op jit(solution)/shard_map/ppermute | solution.py:17
  13.8 8.8 %copy-start.49 = (bf16[20,128,128]{2,1,0:T(8,128)(2,1)S(1)}, bf16[20,128,128]{2,1,0:T(8,128)(2,1)}, u32[]{:S(2)}) copy-start(bf16[20,128,128]{2,1,0:T(8,128)(2,1)} %param.5) | copy-start | bytes 1966084
  18.5 21.5 %copy-start.45 = (bf16[20,140,6]{2,1,0:T(8,128)(2,1)}, bf16[20,140,6]{2,1,0:T(8,128)(2,1)S(1)}, u32[]{:S(2)}) copy-start(bf16[20,140,6]{2,1,0:T(8,128)(2,1)S(1)} %rev.22) | copy-start | bytes 100804
  22.7 17.3 %copy-start.47 = (bf16[20,140,6]{2,1,0:T(8,128)(2,1)}, bf16[20,140,6]{2,1,0:T(8,128)(2,1)S(1)}, u32[]{:S(2)}) copy-start(bf16[20,140,6]{2,1,0:T(8,128)(2,1)S(1)} %rev.26) | copy-start | bytes 100804
  84.7 10.7 %copy-start.44 = (bf16[2,20,128,128]{3,2,1,0:T(8,128)(2,1)}, bf16[2,20,128,128]{3,2,1,0:T(8,128)(2,1)S(1)}, u32[]{:S(2)}) copy-start(bf16[2,20,128,128]{3,2,1,0:T(8,128)(2,1)S(1)} %add_convert_fusion) | copy-start | bytes 3932164
  84.8 7.0 %collective-permute-start.3 = (bf16[2,20,3,128]{3,2,1,0:T(4,128)(2,1)S(1)}, bf16[2,20,3,128]{3,2,1,0:T(4,128)(2,1)S(1)}, u32[]{:S(2)}, u32[]{:S(2)}) collective-permute-start(bf16[2,20,3,128]{3,2,1,0:T(4,128)(2,1)S(1)} %get-tuple-element.160), channel_id=1, source_target_pairs={{0,1},{2,3},{4,5},{6,7},{8,9},{10,11},{12,13},{14,15},{16,17},{18,... | collective-permute-start | bytes 92168 | tf_op jit(solution)/shard_map/ppermute | solution.py:25
  89.2 6.3 %collective-permute-start.4 = (bf16[2,20,3,128]{3,2,1,0:T(4,128)(2,1)S(1)}, bf16[2,20,3,128]{3,2,1,0:T(4,128)(2,1)S(1)}, u32[]{:S(2)}, u32[]{:S(2)}) collective-permute-start(bf16[2,20,3,128]{3,2,1,0:T(4,128)(2,1)S(1)} %get-tuple-element.161), channel_id=1, source_target_pairs={{1,0},{3,2},{5,4},{7,6},{9,8},{11,10},{13,12},{15,14},{17,16},{19,... | collective-permute-start | bytes 92168 | tf_op jit(solution)/shard_map/ppermute | solution.py:28
  188.5 2.8 copy-start.29
  188.5 3.7 %copy-start.27 = (f32[134,134,2]{1,0,2:T(8,128)S(1)}, f32[134,134,2]{1,0,2:T(8,128)}, u32[]{:S(2)}) copy-start(f32[134,134,2]{1,0,2:T(8,128)} %get-tuple-element.26) | copy-start | bytes 430948
  188.5 4.5 %copy-start.25 = (f32[134,134,2]{1,0,2:T(8,128)S(1)}, f32[134,134,2]{1,0,2:T(8,128)}, u32[]{:S(2)}) copy-start(f32[134,134,2]{1,0,2:T(8,128)} %get-tuple-element.27) | copy-start | bytes 430948
  245.5 2.8 copy-start.32
  246.3 2.8 copy-start.31
  247.2 2.8 copy-start.51
  247.2 2.8 copy-start.52
  247.2 2.8 copy-start.53
  247.2 2.8 copy-start.54
  247.3 2.8 copy-start.55
  247.3 2.8 copy-start.56
  247.3 2.8 copy-start.57
  247.3 2.8 copy-start.58
  247.3 2.8 copy-start.59
  247.3 2.8 copy-start.60
  247.3 2.8 copy-start.61
  247.3 2.8 copy-start.62
  247.3 2.8 copy-start.63
  247.3 2.8 copy-start.64
  247.4 2.8 copy-start.65
  247.4 2.8 copy-start.66
  284.5 3.9 %copy-start.72 = (f32[1,2,128,128]{3,2,1,0:T(8,128)S(1)}, f32[1,2,128,128]{3,2,1,0:T(8,128)}, u32[]{:S(2)}) copy-start(f32[1,2,128,128]{3,2,1,0:T(8,128)} %get-tuple-element.54) | copy-start | bytes 393220
  289.3 30.5 %all-to-all-start = ((f32[2,128,2,128]{3,2,0,1:T(2,128)}), f32[2,128,2,128]{3,2,0,1:T(2,128)S(1)}, u32[]{:S(2)}, u32[]{:S(2)}) async-start(f32[2,128,2,128]{3,2,0,1:T(2,128)} %copy.14), calls=%async_computation | async-start | bytes 524288 | tf_op jit(solution)/shard_map/all_to_all | solution.py:124
  (47 other events, 108.1 us)
where the time goes:
time: 321 us
  other arithmetic  197 us (61%)
  local copies, waits for them, and re-layouts  74.2 us (23%)
  starting transfers between devices  28.4 us (9%)
  waiting for transfers between devices  20.4 us (6%)
    rev x2, local copies, waits for them, and re-layouts, body(): padded = jnp.pad(extended, ((0, 0), (0, 0), (0, 0), (3, 3)), mode='reflect')  55.2 us
    dot_general x3, other arithmetic, track(): jnp.einsum('pcik,cik->pik', padded, moved, preferred_element_type=jnp.flo...  54.4 us
    unnamed x3, other arithmetic  47.6 us
    add x52, other arithmetic, window_sum(): total = total + lax.slice_in_dim(values, offset, offset + length, axis=axis)  40.6 us
    another operation x2, other arithmetic, body(): ordered = jnp.transpose(jnp.stack([grad_rows, grad_cols]), (0, 2, 1, 3))  38.2 us
    all_to_all x1, starting transfers between devices, body(): lax.all_to_all(ordered, 'ang', split_axis=1, concat_axis=2, tiled=True)  15.4 us
    all_to_all x1, waiting for transfers between devices, body(): lax.all_to_all(ordered, 'ang', split_axis=1, concat_axis=2, tiled=True)  15.1 us
    ppermute x2, starting transfers between devices, padded_2(): lax.ppermute(lax.slice_in_dim(block, block.shape[dim] - width, None, axis...  9.89 us
  transfers between devices with their start and end apart: 6, of which 3 were waited for; matrix products, arithmetic and copies ran while one was open for 21% of the time, Pallas kernels for 0%

commit v1 on v0

v1 whole, which is shorter than its diff:
```python
import functools

import jax
import jax.numpy as jnp
import numpy as np
from jax import lax
from jax.experimental import pallas as pl
from jax.experimental.pallas import tpu as pltpu
from jax.sharding import PartitionSpec as P

CYCLE = 8
SHARPNESS = 12.0
EPSILON = 1e-05

COLS = 128
CH = 20
SLAB = 72
HALO = 8
WIN = SLAB + HALO
HALF = 64
STEP = 9
SHIFTS = 7
HIGHEST = lax.Precision.HIGHEST


def reflect(position):
    position = np.abs(position)
    return np.where(position > COLS - 1, 2 * (COLS - 1) - position, position)


def column_tables():
    col = np.arange(COLS)
    shift = np.zeros((COLS, SHIFTS, COLS), np.float32)
    spread = np.zeros((COLS, SHIFTS, COLS), np.float32)
    for v in range(SHIFTS):
        shift[reflect(col + v - 3), v, col] = 1.0
        for k in range(-3, 4):
            np.add.at(spread, (reflect(col + v - 3 + k), v, col), 1.0)
    band = np.zeros((COLS, COLS), np.float32)
    edge = np.zeros((COLS, COLS), np.float32)
    for k in range(-3, 4):
        seen = col + k
        inside = (seen >= 0) & (seen < COLS)
        band[seen[inside], col[inside]] += 1.0
        edge[reflect(seen[~inside]), col[~inside]] += 1.0
    both = np.block([[band, edge], [edge, band]])
    zero = np.zeros_like(band)
    alone = np.block([[band + edge, zero], [zero, band + edge]])
    own = np.diag((COLS - 0.5 - col) / COLS)
    far = np.zeros((COLS, COLS))
    far[COLS - 1 - col, col] = (col + 0.5) / COLS
    seam = np.block([[own, far], [far, own]])
    flat = (COLS, SHIFTS * COLS)
    return shift.reshape(flat), spread.reshape(flat), both, alone, seam


def row_tables():
    box = np.zeros((88, WIN), np.float32)
    for row in range(3, WIN - 3):
        box[row, row - 3 : row + 4] = 1.0
    tiles = np.zeros((WIN, 16), np.float32)
    rows = np.arange(HALF)
    tiles[rows, rows // 4] = 1.0
    return box, tiles


def bf16(table):
    return jnp.asarray(table, jnp.bfloat16)


def prepare_kernel(meta, slab, halo, shift, spread, box, flats, norms):
    half = meta[0]
    slab_at = pl.multiple_of(8 * (1 - half), 8)
    halo_at = pl.multiple_of(SLAB * half, 8)
    for ch in range(CH):
        moved = jnp.dot(slab[ch], shift[...], preferred_element_type=jnp.float32)
        for v in range(SHIFTS):
            flats[v, ch, pl.ds(slab_at, SLAB), :] = moved[:, v * COLS : (v + 1) * COLS]
        moved = jnp.dot(halo[0, ch], shift[...], preferred_element_type=jnp.float32)
        for v in range(SHIFTS):
            flats[v, ch, pl.ds(halo_at, HALO), :] = moved[:, v * COLS : (v + 1) * COLS]
    squares = jnp.zeros((WIN, COLS), jnp.float32)
    for ch in range(CH):
        image = flats[3, ch]
        squares = squares + image * image
    rows = jnp.dot(box[...], squares, precision=HIGHEST, preferred_element_type=jnp.float32)
    energy = jnp.dot(rows, spread[...], precision=HIGHEST, preferred_element_type=jnp.float32)
    for v in range(SHIFTS):
        norms[v] = lax.rsqrt(energy[:, v * COLS : (v + 1) * COLS] + EPSILON)


def prepare(meta, slab, halo, shift, spread, box):
    vmem = pl.BlockSpec(memory_space=pltpu.VMEM)
    return pl.pallas_call(
        prepare_kernel,
        name="prepare",
        out_shape=(
            jax.ShapeDtypeStruct((SHIFTS, CH, WIN, COLS), jnp.float32),
            jax.ShapeDtypeStruct((SHIFTS, 88, COLS), jnp.float32),
        ),
        in_specs=[pl.BlockSpec(memory_space=pltpu.SMEM)] + [vmem] * 5,
        out_specs=(vmem, vmem),
    )(meta, slab, halo, shift, spread, box)


def split(values):
    high = values.astype(jnp.bfloat16)
    low = (values - high.astype(jnp.float32)).astype(jnp.bfloat16)
    return high, low


def box_rows(load):
    rows = [load(t) for t in range(STEP + 6)]
    pairs = [rows[i] + rows[i + 1] for i in range(STEP + 4)]
    fours = [pairs[i] + pairs[i + 2] for i in range(STEP)]
    return [(fours[t] + pairs[t + 4]) + rows[t + 6] for t in range(STEP)]


def track_kernel(
    order, meta, own, got, own_halo, got_halo, flats, norms, seam, both, alone, tiles, before,
    out, padded, peaks, products, squares, high, low, high0, low0, window, window0, staged,
):
    half = meta[0]
    slab_at = pl.multiple_of(8 * (1 - half), 8)
    halo_at = pl.multiple_of(SLAB * half, 8)

    def stitch(own_rows, got_rows, at, count):
        for ch in range(CH):
            rows = jnp.concatenate([own_rows(ch), got_rows(ch)], axis=1)
            blended = jnp.dot(rows, seam[...], preferred_element_type=jnp.float32)
            blended = blended.astype(jnp.bfloat16).astype(jnp.float32)
            padded[0, ch, pl.ds(at, count), :] = blended[:, :COLS]
            padded[1, ch, pl.ds(at, count), :] = blended[:, COLS:]

    stitch(lambda ch: own[0, ch], lambda ch: got[ch], slab_at, SLAB)
    stitch(lambda ch: own_halo[0, ch], lambda ch: got_halo[0, ch], halo_at, HALO)
    for d in range(2):
        for j, source in enumerate((own[0, CH, d * 16 : d * 16 + 16], got[CH, d * 16 : d * 16 + 16])):
            peaks[j, d] = jnp.dot(tiles[...], source, preferred_element_type=jnp.float32)

    def multiply(t, carry):
        for v in range(SHIFTS):
            sums = [[None, None] for _ in range(SHIFTS)]
            for ch in range(CH):
                image = [padded[j, ch, pl.ds(t + 5, 8, stride=STEP), :] for j in range(2)]
                for u in range(SHIFTS):
                    moved = flats[v, ch, pl.ds(t + 2 + u, 8, stride=STEP), :]
                    for j in range(2):
                        term = image[j] * moved
                        sums[u][j] = term if ch == 0 else sums[u][j] + term
            for u in range(SHIFTS):
                for j in range(2):
                    products[v, u, j, pl.ds(t, 8, stride=STEP), :] = sums[u][j]
        for j in range(2):
            total = None
            for ch in range(CH):
                image = padded[j, ch, pl.ds(t + 5, 8, stride=STEP), :]
                total = image * image if ch == 0 else total + image * image
            squares[j, pl.ds(t, 8, stride=STEP), :] = total
        return carry

    lax.fori_loop(0, STEP, multiply, 0)

    blank = jnp.zeros((8, COLS), jnp.float32)

    def box(u, carry):
        for v in range(SHIFTS):
            sums = [
                box_rows(lambda t, j=j: products[v, u, j, pl.ds(t, 8, stride=STEP), :]) for j in range(2)
            ]
            if v == 3:
                for j in range(2):
                    one, two = split(jnp.concatenate(sums[j] + [blank], axis=0))
                    at = pl.ds(pl.multiple_of(u * 80, 16), 80)
                    high0[at, j * COLS : (j + 1) * COLS] = one
                    low0[at, j * COLS : (j + 1) * COLS] = two
            else:
                one, two = split(jnp.concatenate(sums[0] + sums[1], axis=0))
                at = pl.ds(pl.multiple_of(u * 144, 16), 144)
                pair, side = (v, 0) if v < 3 else (6 - v, 1)
                high[pair, at, side * COLS : (side + 1) * COLS] = one
                low[pair, at, side * COLS : (side + 1) * COLS] = two
        return carry

    lax.fori_loop(0, SHIFTS, box, 0)
    for j in range(2):
        sums = box_rows(lambda t, j=j: squares[j, pl.ds(t, 8, stride=STEP), :])
        one, two = split(jnp.concatenate(sums + [blank], axis=0))
        high0[560:640, j * COLS : (j + 1) * COLS] = one
        low0[560:640, j * COLS : (j + 1) * COLS] = two

    for pair in range(3):
        window[pair] = jnp.dot(
            high[pair], both[...], preferred_element_type=jnp.float32
        ) + jnp.dot(low[pair], both[...], preferred_element_type=jnp.float32)
    window0[...] = jnp.dot(high0[...], alone[...], preferred_element_type=jnp.float32) + jnp.dot(
        low0[...], alone[...], preferred_element_type=jnp.float32
    )

    def choose(peak_is, candidates):
        chosen = candidates[4]
        for peak in range(4):
            chosen = jnp.where(peak_is[peak], candidates[peak], chosen)
        return chosen

    def score(t, carry):
        for j in range(2):
            peak = [peaks[j, d, pl.ds(t, 8, stride=STEP), :] for d in range(2)]
            row_is = [peak[0] == float(p - 2) for p in range(4)]
            col_is = [peak[1] == float(p - 2) for p in range(4)]
            at = pl.multiple_of(t * 8, 8)
            energy = window0[pl.ds(560 + at, 8), j * COLS : (j + 1) * COLS]
            scale = lax.rsqrt(energy + EPSILON) * SHARPNESS
            near = [[] for _ in range(3)]
            for v in range(SHIFTS):
                scaled = []
                for u in range(SHIFTS):
                    if v == 3:
                        value = window0[pl.ds(u * 80 + at, 8), j * COLS : (j + 1) * COLS]
                    else:
                        pair, side = (v, 0) if v < 3 else (6 - v, 1)
                        value = window[pair, pl.ds(u * 144 + j * 72 + at, 8), side * COLS : (side + 1) * COLS]
                    scaled.append(value * norms[v, pl.ds(t + 5 + u, 8, stride=STEP), :])
                for a in range(3):
                    near[a].append(choose(row_is, scaled[a : a + 5]))
            weight = [
                [jnp.exp(choose(col_is, near[a][b : b + 5]) * scale) for b in range(3)] for a in range(3)
            ]
            by_row = [(weight[a][0] + weight[a][1]) + weight[a][2] for a in range(3)]
            by_col = [(weight[0][b] + weight[1][b]) + weight[2][b] for b in range(3)]
            total = (by_row[0] + by_row[1]) + by_row[2]
            place = order[2 + j]
            staged[pl.ds(8 * t + place, 8, stride=8 * STEP), :] = peak[0] + (by_row[2] - by_row[0]) / total
            staged[pl.ds(8 * t + 4 + place, 8, stride=8 * STEP), :] = peak[1] + (by_col[2] - by_col[0]) / total
        return carry

    if before is not None:
        staged[0 : 8 * HALF, :] = before[...]
    lax.fori_loop(0, STEP, score, 0)
    out[...] = staged[0 : 8 * HALF, :]


def track(order, meta, own, got, own_halo, got_halo, tables, before, chunk):
    flats, norms, seam, both, alone, tiles = tables
    whole = lambda array: pl.BlockSpec(array.shape, lambda i, order, meta: (0,) * array.ndim)
    in_specs = [
        pl.BlockSpec((1, CH + 1, SLAB, COLS), lambda i, order, meta: (order[0], 0, 0, 0)),
        whole(got),
        pl.BlockSpec((1, CH, HALO, COLS), lambda i, order, meta: (order[0], 0, 0, 0)),
        pl.BlockSpec((1, CH, HALO, COLS), lambda i, order, meta: (chunk, 0, 0, 0)),
    ] + [whole(table) for table in tables]
    operands = [own, got, own_halo, got_halo, *tables]
    kernel = track_kernel
    if before is None:
        kernel = lambda *refs: track_kernel(*refs[:12], None, *refs[12:])
    else:
        in_specs.append(whole(before))
        operands.append(before)
    return pl.pallas_call(
        kernel,
        name="track",
        out_shape=jax.ShapeDtypeStruct((8 * HALF, COLS), jnp.float32),
        grid_spec=pltpu.PrefetchScalarGridSpec(
            num_scalar_prefetch=2,
            grid=(1,),
            in_specs=in_specs,
            out_specs=pl.BlockSpec((8 * HALF, COLS), lambda i, order, meta: (0, 0)),
            scratch_shapes=[
                pltpu.VMEM((2, CH, WIN, COLS), jnp.float32),
                pltpu.VMEM((2, 2, WIN, COLS), jnp.float32),
                pltpu.VMEM((SHIFTS, SHIFTS, 2, WIN, COLS), jnp.float32),
                pltpu.VMEM((2, WIN, COLS), jnp.float32),
                pltpu.VMEM((3, 1008, 2 * COLS), jnp.bfloat16),
                pltpu.VMEM((3, 1008, 2 * COLS), jnp.bfloat16),
                pltpu.VMEM((640, 2 * COLS), jnp.bfloat16),
                pltpu.VMEM((640, 2 * COLS), jnp.bfloat16),
                pltpu.VMEM((3, 1008, 2 * COLS), jnp.float32),
                pltpu.VMEM((640, 2 * COLS), jnp.float32),
                pltpu.VMEM((8 * SLAB, COLS), jnp.float32),
            ],
        ),
    )(order, meta, *operands)


def finish_kernel(total, sources, arrived, out):
    sums = arrived[0:8, :]
    for source in range(1, sources):
        sums = sums + arrived[8 * source : 8 * source + 8, :]
    col = lax.broadcasted_iota(jnp.int32, (8, COLS), 1)
    reach = jnp.minimum(col + CYCLE, COLS - 1) - jnp.maximum(col - CYCLE, 0) + 1
    for d in range(2):
        mean = jnp.sum(sums[4 * d : 4 * d + 4], axis=0, keepdims=True) / total
        mean = jnp.broadcast_to(mean, (8, COLS))
        smooth = mean
        for offset in range(1, CYCLE + 1):
            left = pltpu.roll(mean, offset, 1)
            right = pltpu.roll(mean, COLS - offset, 1)
            smooth = smooth + jnp.where(col >= offset, left, 0.0)
            smooth = smooth + jnp.where(col < COLS - offset, right, 0.0)
        ripple = mean - smooth / reach.astype(jnp.float32)
        for side in range(2):
            for q in range(2):
                for m in range(sources // 8):
                    rows = arrived[pl.ds(64 * m + 4 * d + 2 * side + q, 8, stride=8), :]
                    at = 2 * sources * side + 16 * m + q
                    out[d, pl.ds(at, 8, stride=2), :] = rows - ripple


def finish(arrived, projections):
    sources = projections // 4
    vmem = pl.BlockSpec(memory_space=pltpu.VMEM)
    return pl.pallas_call(
        functools.partial(finish_kernel, float(projections), sources),
        name="finish",
        out_shape=jax.ShapeDtypeStruct((2, projections, COLS), jnp.float32),
        in_specs=[vmem],
        out_specs=vmem,
    )(arrived)


def pack(sample, rows, peaks, part):
    slab = lax.dynamic_slice_in_dim(sample, rows, SLAB, axis=2)
    half_peaks = lax.dynamic_slice_in_dim(peaks, part * 16, 16, axis=2)
    half_peaks = jnp.transpose(half_peaks, (1, 0, 2, 3)).reshape(2, 1, 32, COLS)
    half_peaks = jnp.pad(half_peaks, ((0, 0), (0, 0), (0, SLAB - 32), (0, 0)))
    return jnp.concatenate([slab, half_peaks], axis=1)


def body(sample, flat_speckle, peak_shift, partner):
    ang = lax.axis_size("ang")
    pairs = ang // 2
    half = (lax.axis_index("ang") // pairs).astype(jnp.int32)
    swap = (partner[0] % 2).astype(jnp.int32)
    order = [jnp.where(half == 0, k, k ^ swap) for k in range(2)]
    peaks = peak_shift[:, :, ::4, :].astype(jnp.bfloat16)
    route = [(i, (i + pairs) % ang) for i in range(ang)]

    send = pack(sample, 56 * (1 - half), peaks, 1 - half)
    got = [
        lax.ppermute(lax.dynamic_index_in_dim(send, order[k], 0, keepdims=False), "ang", route)
        for k in range(2)
    ]
    border = jnp.concatenate([sample, flat_speckle[None]], axis=0)
    straight = [(2 * i, 2 * i + 1) for i in range(pairs)] + [(2 * i + 1, 2 * i) for i in range(pairs, ang)]
    own_halo = lax.ppermute(
        lax.dynamic_slice_in_dim(border, 120 * (1 - half), HALO, axis=2), ("ang", "row"), straight
    )
    across = [(2 * i, 2 * (i - pairs) + 1) for i in range(pairs, ang)]
    across = across + [(2 * i + 1, 2 * (i + pairs)) for i in range(pairs)]
    edge = lax.dynamic_slice_in_dim(sample, 120 * half, HALO, axis=2)
    edge = jnp.where(order[0] == 0, edge, edge[::-1])
    got_halo = lax.ppermute(edge, ("ang", "row"), across)

    own = pack(sample, 56 * half, peaks, half)
    meta = half[None]
    shift, spread, both, alone, seam = column_tables()
    box, tiles = row_tables()
    flat_slab = lax.dynamic_slice_in_dim(flat_speckle, 56 * half, SLAB, axis=1)
    flats, norms = prepare(
        meta, flat_slab, own_halo[2:], bf16(shift), jnp.asarray(spread), jnp.asarray(box)
    )
    tables = (flats, norms, bf16(seam), bf16(both), bf16(alone), bf16(tiles))
    grads = None
    for k in range(2):
        low, high = jnp.int32(k), 2 + (k ^ swap)
        places = jnp.where(half == 0, jnp.stack([low, high]), jnp.stack([high, low]))
        steer = jnp.concatenate([order[k][None], order[k][None], places]).astype(jnp.int32)
        grads = track(steer, meta, own, got[k], own_halo, got_halo, tables, grads, k)

    groups = [list(range(pairs)), list(range(pairs, ang))]
    arrived = lax.all_to_all(
        grads.reshape(HALF, 8, COLS), "ang", 0, 0, axis_index_groups=groups, tiled=True
    )
    projections = 2 * ang
    sinogram = finish(arrived.reshape(8 * HALF, COLS), projections)
    return sinogram.reshape(2, 1, projections, COLS)


def solution(mesh):
    in_specs = (
        P("ang", None, "row", None),
        P(None, "row", None),
        P(None, "ang", "row", None),
        P("ang"),
    )
    out_specs = P(None, ("row", "ang"), None, None)
    return jax.shard_map(body, mesh=mesh, in_specs=in_specs, out_specs=out_specs, check_vma=False)
```

time: 321 us -> 82.6 us (0.26)
  other arithmetic: 197 us -> 2.77 us
  local copies, waits for them, and re-layouts: 74.2 us -> 4.24 us
  Pallas kernels: 0 us -> 36.3 us
  blocking collectives: 0 us -> 27.5 us
  waiting for transfers between devices: 20.4 us -> 0.01 us
  starting transfers between devices: 28.4 us -> 9.18 us
    rev x5 -> x0, local copies, waits for them, and re-layouts: 67.3 us -> none  [the longest x2 55.2 us: body(): padded = jnp.pad(extended, ((0, 0), (0, 0), (0, 0), (3, 3)), mode='reflect')]
    dot_general x5 -> x0, other arithmetic: 57.1 us -> none  [the longest x3 54.4 us: track(): jnp.einsum('pcik,cik->pik', padded, moved, preferred_element_type=jnp.flo...]
    unnamed x3 -> x0, other arithmetic: 47.6 us -> none
    add x55 -> x0, other arithmetic: 44.4 us -> none  [the longest x52 40.6 us: window_sum(): total = total + lax.slice_in_dim(values, offset, offset + length, axis=axis)]
    another operation x2 -> x1, other arithmetic: 38.2 us -> 0.02 us  [body(): ordered = jnp.transpose(jnp.stack([grad_rows, grad_cols]), (0, 2, 1, 3))]
    pallas_call x0 -> x4, Pallas kernels: none -> 36.3 us  [the longest x2 28.7 us: track(): pl.pallas_call(kernel, name='track', out_shape=jax.ShapeDtypeStruct((8 *...]
    all_to_all x0 -> x1, blocking collectives: none -> 27.5 us  [body(): lax.all_to_all(grads.reshape(HALF, 8, COLS), 'ang', 0, 0, axis_index_grou...]
    all_to_all x1 -> x0, starting transfers between devices: 15.4 us -> none  [body(): lax.all_to_all(ordered, 'ang', split_axis=1, concat_axis=2, tiled=True)]
  transfers between devices with their start and end apart: 6 -> 4, of which waited for: 3 -> 0; matrix products, arithmetic and copies ran while one was open for 21% -> 5% of each run, Pallas kernels for 0% -> 24%
where the time goes in v1:
time: 82.6 us; the launch traced here: 82.3 us
  Pallas kernels  36.3 us (44%)
  blocking collectives  27.5 us (33%)
  starting transfers between devices  9.18 us (11%)
  local copies, waits for them, and re-layouts  4.24 us (5%)
  other arithmetic  2.77 us (3%)
  between operations  2.24 us (3%)
    pallas_call x2, Pallas kernels, track(): pl.pallas_call(kernel, name='track', out_shape=jax.ShapeDtypeStruct((8 *...  28.7 us
    all_to_all x1, blocking collectives, body(): lax.all_to_all(grads.reshape(HALF, 8, COLS), 'ang', 0, 0, axis_index_grou...  27.5 us
    ppermute x1, starting transfers between devices, body(): lax.ppermute(lax.dynamic_slice_in_dim(border, 120 * (1 - half), HALO, axi...  6.97 us
    pallas_call x1, Pallas kernels, prepare(): pl.pallas_call(prepare_kernel, name='prepare', out_shape=(jax.ShapeDtypeS...  5.74 us
    pallas_call x1, Pallas kernels, finish(): pl.pallas_call(functools.partial(finish_kernel, float(projections), sourc...  1.87 us
  transfers between devices with their start and end apart: 4, of which 0 were waited for; matrix products, arithmetic and copies ran while one was open for 5% of the time, Pallas kernels for 24%

profile of v1, /device:TPU:1, one launch (start us, length us, event | category | flops | bytes accessed | tf_op | source)
XLA Modules:
  0.0 82.3 jit_solution(12838601336609428969)
XLA Ops:
  2.0 0.0 copy-start
  2.0 1.0 %constant_dynamic-slice_fusion.1 = bf16[2,20,8,128]{3,2,1,0:T(8,128)(2,1)S(1)} fusion(bf16[2,20,128,128]{3,2,1,0:T(8,128)(2,1)} %param.11, s32[]{:T(128)S(6)} %select_n.77), kind=kLoop, calls=%fused_computation.18 | loop fusion | bytes 163844 | tf_op jit(solution)/shard_map/dynamic_slice | solution.py:350
  3.1 0.7 collective-permute-start.2
  3.7 0.9 %fusion.6 = bf16[3,20,8,128]{3,2,1,0:T(8,128)(2,1)S(1)} fusion(s32[]{:T(128)S(6)} %select_n.74, bf16[2,20,128,128]{3,2,1,0:T(8,128)(2,1)} %param.11, bf16[1,20,128,128]{3,2,1,0:T(8,128)(2,1)} %bitcast.25), kind=kLoop, calls=%fused_computation.14 | loop fusion | flops 245760 | bytes 2088964 | tf_op jit(solution)/shard_map/concatenate | solution.py:343
  4.6 7.0 %collective-permute-start.1 = (bf16[3,20,8,128]{3,2,1,0:T(8,128)(2,1)S(1)}, bf16[3,20,8,128]{3,2,1,0:T(8,128)(2,1)S(1)}, u32[]{:S(2)}, u32[]{:S(2)}) collective-permute-start(bf16[3,20,8,128]{3,2,1,0:T(8,128)(2,1)S(1)} %fusion.6), channel_id=1, source_target_pairs={{0,1},{2,3},{4,5},{6,7},{8,9},{10,11},{12,13},{14,15},{16,17},{18,... | collective-permute-start | bytes 368648 | tf_op jit(solution)/shard_map/ppermute | solution.py:345
  11.7 0.1 slice.11
  11.9 0.0 copy-start.1
  11.9 0.2 constant_dynamic-slice_fusion.3
  12.1 0.1 fusion.3
  12.2 0.1 collective-permute-start.3
  12.3 1.5 %collective-permute-start = (bf16[21,72,128]{2,1,0:T(8,128)(2,1)S(1)}, bf16[21,72,128]{2,1,0:T(8,128)(2,1)S(1)}, u32[]{:S(2)}, u32[]{:S(2)}) collective-permute-start(bf16[21,72,128]{2,1,0:T(8,128)(2,1)S(1)} %get-tuple-element.12), channel_id=1, source_target_pairs={{0,128},{2,130},{4,132},{6,134},{8,136},{10,138},{12,140},{14,142}... | collective-permute-start | bytes 1161224 | tf_op jit(solution)/shard_map/ppermute | solution.py:340
  13.7 0.0 copy-done.1
  13.7 0.8 constant_dynamic-slice_fusion.slab
  14.5 0.1 broadcast_select_fusion.1
  14.6 0.9 %fusion.1.refs_2_.own = bf16[2,21,72,128]{3,2,1,0:T(8,128)(2,1)} fusion(bf16[2,1,32,128]{3,2,1,0:T(8,128)(2,1)S(1)} %bitcast.28, bf16[2,20,72,128]{3,2,1,0:T(8,128)(2,1)S(1)} %get-tuple-element.10), kind=kLoop, calls=%fused_computation.6 | loop fusion | flops 2322432 | bytes 1527808 | tf_op jit(solution)/shard_map/concatenate | solution.py:326
  15.5 0.1 broadcast_select_fusion
  15.6 0.7 pad_add_fusion
  16.2 0.0 collective-permute-done.1.refs_4_.own_halo
  16.3 0.7 slice.13.halo
  16.9 5.7 %prepare.1 = (f32[7,20,80,128]{3,2,1,0:T(8,128)}, f32[7,88,128]{2,1,0:T(8,128)}) custom-call(s32[1]{0:T(128)} %bitcast.3.meta.refs_1_, bf16[20,72,128]{2,1,0:T(8,128)(2,1)} %constant_dynamic-slice_fusion.slab, bf16[1,20,8,128]{3,2,1,0:T(8,128)(2,1)} %slice.13.halo, bf16[128,896]{1,0:T(8,128)(2,1)} %constant.71.clone.shift, ...), custom_call_target="tpu_custom_call" | custom-call | tf_op jit(solution)/shard_map/prepare/pallas_call | solution.py:94
  22.7 0.0 collective-permute-done.2.refs_5_.got_halo
  22.7 0.0 collective-permute-done.3.refs_3_
  22.7 0.0 copy-start.4
  22.7 0.0 copy-done.2
  22.7 0.6 copy-done.5
  23.3 0.1 copy-done.4
  23.4 14.4 %track.2.before = f32[512,128]{1,0:T(8,128)} custom-call(s32[4]{0:T(128)} %get-tuple-element.16.refs_0_, s32[1]{0:T(128)} %bitcast.3.meta.refs_1_, bf16[2,21,72,128]{3,2,1,0:T(8,128)(2,1)} %fusion.1.refs_2_.own, bf16[21,72,128]{2,1,0:T(8,128)(2,1)} %copy-done.4, bf16[3,20,8,128]{3,2,1,0:T(8,128)(2,1)} %copy-done.2, bf16[2,20,8,128]{3,2,1,0:T(8,128)(2,1)} %copy-done.5, ...), custom_call_target="tpu_custom_call" | custom-call | tf_op jit(solution)/shard_map/track/pallas_call | solution.py:259
  37.8 0.0 collective-permute-done.got
  37.8 0.7 copy-done.3
  38.5 14.4 %track.3 = f32[512,128]{1,0:T(8,128)} custom-call(s32[4]{0:T(128)} %get-tuple-element.15.order, s32[1]{0:T(128)} %bitcast.3.meta.refs_1_, bf16[2,21,72,128]{3,2,1,0:T(8,128)(2,1)} %fusion.1.refs_2_.own, bf16[21,72,128]{2,1,0:T(8,128)(2,1)} %copy-done.3, bf16[3,20,8,128]{3,2,1,0:T(8,128)(2,1)} %copy-done.2, bf16[2,20,8,128]{3,2,1,0:T(8,128)(2,1)} %copy-done.5, ...), custom_call_target="tpu_custom_call" | custom-call | tf_op jit(solution)/shard_map/track/pallas_call | solution.py:259
  52.9 27.5 %all_to_all.5 = f32[64,8,128]{2,1,0:T(8,128)} all-to-all(f32[64,8,128]{2,1,0:T(8,128)} %bitcast.27), channel_id=1, replica_groups={{0,2,4,6,8,10,12,14,16,18,20,22,24,26,28,30,32,34,36,38,40,42,44,46,48,..., dimensions={0} | all-to-all | bytes 524288 | tf_op jit(solution)/shard_map/all_to_all | solution.py:371
  80.4 1.9 %finish.1 = f32[2,256,128]{2,1,0:T(8,128)} custom-call(f32[512,128]{1,0:T(8,128)} %bitcast.26), custom_call_target="tpu_custom_call" | custom-call | tf_op jit(solution)/shard_map/finish/pallas_call | solution.py:312
  (10 shorter events, 0.1 us)
Async XLA Ops:
  0.0 11.7 %copy-start.6 = (s32[2,2,128,128]{3,2,1,0:T(8,128)S(1)}, s32[2,2,128,128]{3,2,1,0:T(8,128)}, u32[]{:S(2)}) copy-start(s32[2,2,128,128]{3,2,1,0:T(8,128)} %param.13) | copy-start | bytes 786436
  2.0 9.9 %copy-start = (bf16[2,20,128,128]{3,2,1,0:T(8,128)(2,1)S(1)}, bf16[2,20,128,128]{3,2,1,0:T(8,128)(2,1)}, u32[]{:S(2)}) copy-start(bf16[2,20,128,128]{3,2,1,0:T(8,128)(2,1)} %param.11) | copy-start | bytes 3932164
  3.1 19.6 %collective-permute-start.2 = (bf16[2,20,8,128]{3,2,1,0:T(8,128)(2,1)S(1)}, bf16[2,20,8,128]{3,2,1,0:T(8,128)(2,1)S(1)}, u32[]{:S(2)}, u32[]{:S(2)}) collective-permute-start(bf16[2,20,8,128]{3,2,1,0:T(8,128)(2,1)S(1)} %reverse_select_fusion), channel_id=1, source_target_pairs={{128,1},{130,3},{132,5},{134,7},{136,9},{138,11},{140,13},{142,15}... | collective-permute-start | bytes 245768 | tf_op jit(solution)/shard_map/ppermute | solution.py:352
  4.6 11.6 %collective-permute-start.1 = (bf16[3,20,8,128]{3,2,1,0:T(8,128)(2,1)S(1)}, bf16[3,20,8,128]{3,2,1,0:T(8,128)(2,1)S(1)}, u32[]{:S(2)}, u32[]{:S(2)}) collective-permute-start(bf16[3,20,8,128]{3,2,1,0:T(8,128)(2,1)S(1)} %fusion.6), channel_id=1, source_target_pairs={{0,1},{2,3},{4,5},{6,7},{8,9},{10,11},{12,13},{14,15},{16,17},{18,... | collective-permute-start | bytes 368648 | tf_op jit(solution)/shard_map/ppermute | solution.py:345
  11.9 1.8 %copy-start.1 = (bf16[20,128,128]{2,1,0:T(8,128)(2,1)S(1)}, bf16[20,128,128]{2,1,0:T(8,128)(2,1)}, u32[]{:S(2)}) copy-start(bf16[20,128,128]{2,1,0:T(8,128)(2,1)} %param.12) | copy-start | bytes 1966084
  12.2 10.5 %collective-permute-start.3 = (bf16[21,72,128]{2,1,0:T(8,128)(2,1)S(1)}, bf16[21,72,128]{2,1,0:T(8,128)(2,1)S(1)}, u32[]{:S(2)}, u32[]{:S(2)}) collective-permute-start(bf16[21,72,128]{2,1,0:T(8,128)(2,1)S(1)} %get-tuple-element.11), channel_id=1, source_target_pairs={{0,128},{2,130},{4,132},{6,134},{8,136},{10,138},{12,140},{14,142}... | collective-permute-start | bytes 1161224 | tf_op jit(solution)/shard_map/ppermute | solution.py:340
  12.3 25.5 %collective-permute-start = (bf16[21,72,128]{2,1,0:T(8,128)(2,1)S(1)}, bf16[21,72,128]{2,1,0:T(8,128)(2,1)S(1)}, u32[]{:S(2)}, u32[]{:S(2)}) collective-permute-start(bf16[21,72,128]{2,1,0:T(8,128)(2,1)S(1)} %get-tuple-element.12), channel_id=1, source_target_pairs={{0,128},{2,130},{4,132},{6,134},{8,136},{10,138},{12,140},{14,142}... | collective-permute-start | bytes 1161224 | tf_op jit(solution)/shard_map/ppermute | solution.py:340
  16.3 6.4 %copy-start.2 = (bf16[3,20,8,128]{3,2,1,0:T(8,128)(2,1)}, bf16[3,20,8,128]{3,2,1,0:T(8,128)(2,1)S(1)}, u32[]{:S(2)}) copy-start(bf16[3,20,8,128]{3,2,1,0:T(8,128)(2,1)S(1)} %collective-permute-done.1.refs_4_.own_halo) | copy-start | bytes 368644
  22.7 0.6 copy-start.5
  22.7 0.8 copy-start.4
  37.8 0.7 copy-start.3

commit v2 on v1

v2 whole, which is shorter than its diff:
```python
import functools

import jax
import jax.numpy as jnp
from jax import lax
from jax.experimental import pallas as pl
from jax.experimental.pallas import tpu as pltpu
from jax.sharding import PartitionSpec as P


CYCLE = 8
SHARPNESS = 12.0
EPSILON = 1e-05

COLS = 128
CH = 20
SLAB = 72
HALO = 8
WIN = SLAB + HALO
HALF = 64
STEP = 9
SHIFTS = 7
HIGHEST = lax.Precision.HIGHEST


SMEM = pl.BlockSpec(memory_space=pltpu.SMEM)
VMEM = pl.BlockSpec(memory_space=pltpu.VMEM)
HBM = pl.BlockSpec(memory_space=pltpu.HBM)


def pack_kernel(code, sample, flat, peaks, send_0, send_1, straight, across, tall, sems):
    half, swap = code[0] & 1, code[0] >> 1
    other = 1 - half
    first = half * swap
    slab_at = pl.multiple_of(56 * other, 8)
    halo_at = pl.multiple_of(120 * other, 8)
    edge_at = pl.multiple_of(120 * half, 8)
    tall_at = pl.multiple_of(HALF * other, 8)
    copies = [
        (peaks.at[:, :, pl.ds(tall_at, HALF), :], tall),
        (sample.at[:, :, pl.ds(halo_at, HALO), :], straight.at[0:2]),
        (flat.at[:, pl.ds(halo_at, HALO), :], straight.at[2]),
        (sample.at[first, :, pl.ds(slab_at, SLAB), :], send_0.at[0:CH]),
        (sample.at[1 - first, :, pl.ds(slab_at, SLAB), :], send_1.at[0:CH]),
        (sample.at[first, :, pl.ds(edge_at, HALO), :], across.at[0]),
        (sample.at[1 - first, :, pl.ds(edge_at, HALO), :], across.at[1]),
    ]
    copies = [pltpu.make_async_copy(a, b, sems.at[i]) for i, (a, b) in enumerate(copies)]
    for copy in copies:
        copy.start()
    copies[0].wait()
    for send, index in ((send_0, first), (send_1, 1 - first)):
        rows = [tall[d, index, pl.ds(0, 16, stride=4), :] for d in range(2)]
        rows = rows + [jnp.zeros((SLAB - 32, COLS), jnp.int32)]
        send[CH] = jnp.concatenate(rows, axis=0).astype(jnp.float32).astype(jnp.bfloat16)
    for copy in copies[1:]:
        copy.wait()


def pack(code, sample, flat, peaks):
    image = lambda *shape: jax.ShapeDtypeStruct((*shape, COLS), jnp.bfloat16)
    return pl.pallas_call(
        pack_kernel,
        name="pack",
        out_shape=(
            image(CH + 1, SLAB), image(CH + 1, SLAB), image(3, CH, HALO), image(2, CH, HALO),
        ),
        in_specs=[SMEM, HBM, HBM, HBM],
        out_specs=(VMEM,) * 4,
        scratch_shapes=[pltpu.VMEM((2, 2, HALF, COLS), jnp.int32), pltpu.SemaphoreType.DMA((7,))],
        compiler_params=pltpu.CompilerParams(vmem_limit_bytes=8 << 20),
    )(code, sample, flat, peaks)


def within(a, b, reach):
    return (jnp.abs(a - b) <= reach).astype(jnp.float32)


def seam_tables():
    r = lax.broadcasted_iota(jnp.int32, (COLS, COLS), 0)
    c = lax.broadcasted_iota(jnp.int32, (COLS, COLS), 1)
    last = COLS - 1
    own = jnp.where(r == c, (last - c).astype(jnp.float32) + 0.5, 0.0) / COLS
    far = jnp.where(r == last - c, c.astype(jnp.float32) + 0.5, 0.0) / COLS
    band = within(r, c, 3)
    edge = jnp.where(jnp.logical_and(r >= 1, r + c <= 3), 1.0, 0.0)
    edge = edge + jnp.where(jnp.logical_and(r <= last - 1, r + c >= 2 * last - 3), 1.0, 0.0)
    zero = jnp.zeros_like(band)

    def blocks(a, b):
        rows = [jnp.concatenate([a, b], axis=1), jnp.concatenate([b, a], axis=1)]
        return jnp.concatenate(rows, axis=0)

    return blocks(own, far), blocks(band, edge), blocks(band + edge, zero)


def prepare_kernel(
    code, flat_all, halo, sample, peaks, flats, norms, own, own_peaks, seam, both, alone, tiles, flat, sems
):
    half = code[0] & 1
    tall_at = pl.multiple_of(HALF * half, 8)
    from_row = pl.multiple_of(56 * half, 8)
    copies = [
        (flat_all.at[:, pl.ds(from_row, SLAB), :], flat),
        (sample.at[:, :, pl.ds(from_row, SLAB), :], own),
        (peaks.at[:, :, pl.ds(tall_at, HALF), :], own_peaks),
    ]
    copies = [pltpu.make_async_copy(a, b, sems.at[i]) for i, (a, b) in enumerate(copies)]
    for copy in copies:
        copy.start()
    for ref, table in zip((seam, both, alone), seam_tables()):
        ref[...] = table.astype(jnp.bfloat16)
    row = lax.broadcasted_iota(jnp.int32, (WIN, 16), 0)
    tile = lax.broadcasted_iota(jnp.int32, (WIN, 16), 1)
    tiles[...] = jnp.where(row >> 2 == tile, 1.0, 0.0).astype(jnp.bfloat16)
    slab_at = pl.multiple_of(8 * (1 - half), 8)
    halo_at = pl.multiple_of(SLAB * half, 8)
    last = COLS - 1
    source = lax.broadcasted_iota(jnp.int32, (COLS, COLS), 0)
    target = lax.broadcasted_iota(jnp.int32, (COLS, COLS), 1)
    shift, spread = [], []
    for v in range(-3, 4):
        seen = target + v
        low = jnp.where(source >= 1, -source, -COLS)
        high = jnp.where(source <= last - 1, 2 * last - source, 3 * COLS)
        for tables, reach in ((shift, 0), (spread, 3)):
            table = within(source, seen, reach) + within(low, seen, reach) + within(high, seen, reach)
            tables.append(table.astype(jnp.bfloat16))
    shift = jnp.concatenate(shift, axis=1)
    spread = jnp.concatenate(spread, axis=1)
    copies[0].wait()
    for ch in range(CH):
        moved = jnp.dot(flat[ch], shift, preferred_element_type=jnp.float32)
        for v in range(SHIFTS):
            flats[v, ch, pl.ds(slab_at, SLAB), :] = moved[:, v * COLS : (v + 1) * COLS]
        moved = jnp.dot(halo[2, ch], shift, preferred_element_type=jnp.float32)
        for v in range(SHIFTS):
            flats[v, ch, pl.ds(halo_at, HALO), :] = moved[:, v * COLS : (v + 1) * COLS]
    squares = jnp.zeros((WIN, COLS), jnp.float32)
    for ch in range(CH):
        image = flats[3, ch]
        squares = squares + image * image
    center = lax.broadcasted_iota(jnp.int32, (88, WIN), 0)
    member = lax.broadcasted_iota(jnp.int32, (88, WIN), 1)
    box = within(center, member, 3)
    rows = jnp.dot(box, squares, precision=HIGHEST, preferred_element_type=jnp.float32)
    high, low = split(rows)
    energy = jnp.dot(high, spread, preferred_element_type=jnp.float32) + jnp.dot(
        low, spread, preferred_element_type=jnp.float32
    )
    for v in range(SHIFTS):
        norms[v] = lax.rsqrt(energy[:, v * COLS : (v + 1) * COLS] + EPSILON)
    copies[1].wait()
    copies[2].wait()


def prepare(code, flat, halo, sample, peaks):
    table = lambda *shape: jax.ShapeDtypeStruct(shape, jnp.bfloat16)
    return pl.pallas_call(
        prepare_kernel,
        name="prepare",
        out_shape=(
            jax.ShapeDtypeStruct((SHIFTS, CH, WIN, COLS), jnp.float32),
            jax.ShapeDtypeStruct((SHIFTS, 88, COLS), jnp.float32),
            table(2, CH, SLAB, COLS),
            jax.ShapeDtypeStruct((2, 2, HALF, COLS), jnp.int32),
            table(2 * COLS, 2 * COLS),
            table(2 * COLS, 2 * COLS),
            table(2 * COLS, 2 * COLS),
            table(WIN, 16),
        ),
        in_specs=[SMEM, HBM, VMEM, HBM, HBM],
        out_specs=(VMEM,) * 8,
        scratch_shapes=[pltpu.VMEM((CH, SLAB, COLS), jnp.bfloat16), pltpu.SemaphoreType.DMA((3,))],
        compiler_params=pltpu.CompilerParams(vmem_limit_bytes=16 << 20),
    )(code, flat, halo, sample, peaks)


def split(values):
    high = values.astype(jnp.bfloat16)
    low = (values - high.astype(jnp.float32)).astype(jnp.bfloat16)
    return high, low


def box_rows(load):
    rows = [load(t) for t in range(STEP + 6)]
    pairs = [rows[i] + rows[i + 1] for i in range(STEP + 4)]
    fours = [pairs[i] + pairs[i + 2] for i in range(STEP)]
    return [(fours[t] + pairs[t + 4]) + rows[t + 6] for t in range(STEP)]


def track_kernel(
    chunk, code, own, own_peaks, got, own_halo, got_halo, flats, norms, seam, both, alone, tiles, before,
    out, padded, peaks, products, squares, high, low, high0, low0, window, window0, staged,
):
    half, swap = code[0] & 1, code[0] >> 1
    swapped = chunk ^ swap
    index = jnp.where(half == 0, chunk, swapped)
    places = (jnp.where(half == 0, chunk, 2 + swapped), jnp.where(half == 0, 2 + swapped, chunk))
    slab_at = pl.multiple_of(8 * (1 - half), 8)
    halo_at = pl.multiple_of(SLAB * half, 8)

    def stitch(own_rows, got_rows, at, count):
        for ch in range(CH):
            rows = jnp.concatenate([own_rows(ch), got_rows(ch)], axis=1)
            blended = jnp.dot(rows, seam[...], preferred_element_type=jnp.float32)
            blended = blended.astype(jnp.bfloat16).astype(jnp.float32)
            padded[0, ch, pl.ds(at, count), :] = blended[:, :COLS]
            padded[1, ch, pl.ds(at, count), :] = blended[:, COLS:]

    stitch(lambda ch: own[index, ch], lambda ch: got[ch], slab_at, SLAB)
    stitch(lambda ch: own_halo[index, ch], lambda ch: got_halo[chunk, ch], halo_at, HALO)
    for d in range(2):
        tall = own_peaks[d, index]
        peaks[0, d, 0:HALF, :] = tall.astype(jnp.float32)
        peaks[0, d, HALF:WIN, :] = jnp.zeros((WIN - HALF, COLS), jnp.float32)
        source = got[CH, d * 16 : d * 16 + 16]
        peaks[1, d] = jnp.dot(tiles[...], source, preferred_element_type=jnp.float32)

    def multiply(t, carry):
        for v in range(SHIFTS):
            sums = [[None, None] for _ in range(SHIFTS)]
            for ch in range(CH):
                image = [padded[j, ch, pl.ds(t + 5, 8, stride=STEP), :] for j in range(2)]
                for u in range(SHIFTS):
                    moved = flats[v, ch, pl.ds(t + 2 + u, 8, stride=STEP), :]
                    for j in range(2):
                        term = image[j] * moved
                        sums[u][j] = term if ch == 0 else sums[u][j] + term
            for u in range(SHIFTS):
                for j in range(2):
                    products[v, u, j, pl.ds(t, 8, stride=STEP), :] = sums[u][j]
        for j in range(2):
            total = None
            for ch in range(CH):
                image = padded[j, ch, pl.ds(t + 5, 8, stride=STEP), :]
                total = image * image if ch == 0 else total + image * image
            squares[j, pl.ds(t, 8, stride=STEP), :] = total
        return carry

    lax.fori_loop(0, STEP, multiply, 0)

    blank = jnp.zeros((8, COLS), jnp.float32)

    def box(u, carry):
        for v in range(SHIFTS):
            sums = [
                box_rows(lambda t, j=j: products[v, u, j, pl.ds(t, 8, stride=STEP), :]) for j in range(2)
            ]
            if v == 3:
                for j in range(2):
                    one, two = split(jnp.concatenate(sums[j] + [blank], axis=0))
                    at = pl.ds(pl.multiple_of(u * 80, 16), 80)
                    high0[at, j * COLS : (j + 1) * COLS] = one
                    low0[at, j * COLS : (j + 1) * COLS] = two
            else:
                one, two = split(jnp.concatenate(sums[0] + sums[1], axis=0))
                at = pl.ds(pl.multiple_of(u * 144, 16), 144)
                pair, side = (v, 0) if v < 3 else (6 - v, 1)
                high[pair, at, side * COLS : (side + 1) * COLS] = one
                low[pair, at, side * COLS : (side + 1) * COLS] = two
        return carry

    lax.fori_loop(0, SHIFTS, box, 0)
    for j in range(2):
        sums = box_rows(lambda t, j=j: squares[j, pl.ds(t, 8, stride=STEP), :])
        one, two = split(jnp.concatenate(sums + [blank], axis=0))
        high0[560:640, j * COLS : (j + 1) * COLS] = one
        low0[560:640, j * COLS : (j + 1) * COLS] = two

    for pair in range(3):
        window[pair] = jnp.dot(
            high[pair], both[...], preferred_element_type=jnp.float32
        ) + jnp.dot(low[pair], both[...], preferred_element_type=jnp.float32)
    window0[...] = jnp.dot(high0[...], alone[...], preferred_element_type=jnp.float32) + jnp.dot(
        low0[...], alone[...], preferred_element_type=jnp.float32
    )

    def choose(peak_is, candidates):
        chosen = candidates[4]
        for peak in range(4):
            chosen = jnp.where(peak_is[peak], candidates[peak], chosen)
        return chosen

    def score(t, carry):
        for j in range(2):
            peak = [peaks[j, d, pl.ds(t, 8, stride=STEP), :] for d in range(2)]
            row_is = [peak[0] == float(p - 2) for p in range(4)]
            col_is = [peak[1] == float(p - 2) for p in range(4)]
            at = pl.multiple_of(t * 8, 8)
            energy = window0[pl.ds(560 + at, 8), j * COLS : (j + 1) * COLS]
            scale = lax.rsqrt(energy + EPSILON) * SHARPNESS
            near = [[] for _ in range(3)]
            for v in range(SHIFTS):
                scaled = []
                for u in range(SHIFTS):
                    if v == 3:
                        value = window0[pl.ds(u * 80 + at, 8), j * COLS : (j + 1) * COLS]
                    else:
                        pair, side = (v, 0) if v < 3 else (6 - v, 1)
                        value = window[pair, pl.ds(u * 144 + j * 72 + at, 8), side * COLS : (side + 1) * COLS]
                    scaled.append(value * norms[v, pl.ds(t + 5 + u, 8, stride=STEP), :])
                for a in range(3):
                    near[a].append(choose(row_is, scaled[a : a + 5]))
            weight = [
                [jnp.exp(choose(col_is, near[a][b : b + 5]) * scale) for b in range(3)] for a in range(3)
            ]
            by_row = [(weight[a][0] + weight[a][1]) + weight[a][2] for a in range(3)]
            by_col = [(weight[0][b] + weight[1][b]) + weight[2][b] for b in range(3)]
            total = (by_row[0] + by_row[1]) + by_row[2]
            place = places[j]
            staged[pl.ds(8 * t + place, 8, stride=8 * STEP), :] = peak[0] + (by_row[2] - by_row[0]) / total
            staged[pl.ds(8 * t + 4 + place, 8, stride=8 * STEP), :] = peak[1] + (by_col[2] - by_col[0]) / total
        return carry

    if before is not None:
        staged[0 : 8 * HALF, :] = before[...]
    lax.fori_loop(0, STEP, score, 0)
    out[...] = staged[0 : 8 * HALF, :]


def track(chunk, code, own, own_peaks, got, own_halo, got_halo, tables, before):
    operands = [code, own, own_peaks, got, own_halo, got_halo, *tables]
    if before is None:
        kernel = lambda *refs: track_kernel(chunk, *refs[:12], None, *refs[12:])
    else:
        kernel = functools.partial(track_kernel, chunk)
        operands.append(before)
    return pl.pallas_call(
        kernel,
        name="track",
        out_shape=jax.ShapeDtypeStruct((8 * HALF, COLS), jnp.float32),
        in_specs=[SMEM] + [VMEM] * (len(operands) - 1),
        out_specs=VMEM,
        scratch_shapes=[
            pltpu.VMEM((2, CH, WIN, COLS), jnp.float32),
            pltpu.VMEM((2, 2, WIN, COLS), jnp.float32),
            pltpu.VMEM((SHIFTS, SHIFTS, 2, WIN, COLS), jnp.float32),
            pltpu.VMEM((2, WIN, COLS), jnp.float32),
            pltpu.VMEM((3, 1008, 2 * COLS), jnp.bfloat16),
            pltpu.VMEM((3, 1008, 2 * COLS), jnp.bfloat16),
            pltpu.VMEM((640, 2 * COLS), jnp.bfloat16),
            pltpu.VMEM((640, 2 * COLS), jnp.bfloat16),
            pltpu.VMEM((3, 1008, 2 * COLS), jnp.float32),
            pltpu.VMEM((640, 2 * COLS), jnp.float32),
            pltpu.VMEM((8 * SLAB, COLS), jnp.float32),
        ],
        compiler_params=pltpu.CompilerParams(vmem_limit_bytes=24 << 20),
    )(*operands)


def finish_kernel(total, sources, arrived, out):
    sums = arrived[0:8, :]
    for source in range(1, sources):
        sums = sums + arrived[8 * source : 8 * source + 8, :]
    col = lax.broadcasted_iota(jnp.int32, (8, COLS), 1)
    reach = jnp.minimum(col + CYCLE, COLS - 1) - jnp.maximum(col - CYCLE, 0) + 1
    for d in range(2):
        mean = jnp.sum(sums[4 * d : 4 * d + 4], axis=0, keepdims=True) / total
        mean = jnp.broadcast_to(mean, (8, COLS))
        smooth = mean
        for offset in range(1, CYCLE + 1):
            left = pltpu.roll(mean, offset, 1)
            right = pltpu.roll(mean, COLS - offset, 1)
            smooth = smooth + jnp.where(col >= offset, left, 0.0)
            smooth = smooth + jnp.where(col < COLS - offset, right, 0.0)
        ripple = mean - smooth / reach.astype(jnp.float32)
        for side in range(2):
            for q in range(2):
                for m in range(sources // 8):
                    rows = arrived[pl.ds(64 * m + 4 * d + 2 * side + q, 8, stride=8), :]
                    at = 2 * sources * side + 16 * m + q
                    out[d, pl.ds(at, 8, stride=2), :] = rows - ripple


def finish(arrived, projections):
    sources = projections // 4
    return pl.pallas_call(
        functools.partial(finish_kernel, float(projections), sources),
        name="finish",
        out_shape=jax.ShapeDtypeStruct((2, projections, COLS), jnp.float32),
        in_specs=[VMEM],
        out_specs=VMEM,
        compiler_params=pltpu.CompilerParams(vmem_limit_bytes=8 << 20),
    )(arrived)


def program(sample, flat_speckle, peak_shift, partner):
    ang = lax.axis_size("ang")
    pairs = ang // 2
    half = (lax.axis_index("ang") >= pairs).astype(jnp.int32)
    route = [(i, (i + pairs) % ang) for i in range(ang)]
    straight = [(2 * i, 2 * i + 1) for i in range(pairs)] + [(2 * i + 1, 2 * i) for i in range(pairs, ang)]
    across = [(2 * i, 2 * (i - pairs) + 1) for i in range(pairs, ang)]
    across = across + [(2 * i + 1, 2 * (i + pairs)) for i in range(pairs)]

    code = (half + 2 * (partner[0] & 1))[None]
    sample, flat_speckle, peak_shift = (
        pltpu.with_memory_space_constraint(array, pltpu.HBM) for array in (sample, flat_speckle, peak_shift)
    )
    send_0, send_1, straight_rows, across_rows = pack(code, sample, flat_speckle, peak_shift)
    own_halo = lax.ppermute(straight_rows, ("ang", "row"), straight)
    got_0 = lax.ppermute(send_0, "ang", route)
    got_halo = lax.ppermute(across_rows, ("ang", "row"), across)
    got_1 = lax.ppermute(send_1, "ang", route)

    flats, norms, own, own_peaks, *tables = prepare(code, flat_speckle, own_halo, sample, peak_shift)
    tables = (flats, norms, *tables)
    grads = None
    for k, got in enumerate((got_0, got_1)):
        grads = track(k, code, own, own_peaks, got, own_halo, got_halo, tables, grads)

    groups = [list(range(pairs)), list(range(pairs, ang))]
    arrived = lax.all_to_all(
        grads.reshape(HALF, 8, COLS), "ang", 0, 0, axis_index_groups=groups, tiled=True
    )
    projections = 2 * ang
    sinogram = finish(arrived.reshape(8 * HALF, COLS), projections)
    return sinogram.reshape(2, 1, projections, COLS)


def solution(mesh):
    in_specs = (
        P("ang", None, "row", None),
        P(None, "row", None),
        P(None, "ang", "row", None),
        P("ang"),
    )
    out_specs = P(None, ("row", "ang"), None, None)
    return jax.shard_map(program, mesh=mesh, in_specs=in_specs, out_specs=out_specs, check_vma=False)
```

time: 82.6 us -> 72.8 us (0.88); the launches traced: 82.3 us -> 71.5 us
  waiting for transfers between devices: 0.01 us -> 12.8 us
  Pallas kernels: 36.3 us -> 24 us
  local copies, waits for them, and re-layouts: 4.24 us -> 0 us
  other arithmetic: 2.77 us -> 0 us
  between operations: 2.24 us -> 0.73 us
  starting transfers between devices: 9.18 us -> 7.68 us
  blocking collectives: 27.5 us -> 26.3 us
    ppermute x4, waiting for transfers between devices: 0.01 us -> 12.8 us  [the longest x1 12.8 us: program(): own_halo = lax.ppermute(straight_rows, ('ang', 'row'), straight)]
    pallas_call x2, Pallas kernels: 28.7 us -> 18.1 us  [track(): pl.pallas_call(kernel, name='track', out_shape=jax.ShapeDtypeStruct((8 *...]
    concatenate x3 -> x0, other arithmetic: 2.51 us -> none  [the longest x1 0.95 us: pack(): return jnp.concatenate([slab, half_peaks], axis=1)]
    pallas_call x1, Pallas kernels: 5.74 us -> 3.62 us  [prepare(): pl.pallas_call(prepare_kernel, name='prepare', out_shape=(jax.ShapeDtypeS...]
    dynamic_slice x4 -> x0, local copies, waits for them, and re-layouts: 1.96 us -> none  [the longest x1 0.99 us: body(): edge = lax.dynamic_slice_in_dim(sample, 120 * half, HALO, axis=2)]
    unnamed x14 -> x0, local copies, waits for them, and re-layouts: 1.51 us -> none
    ppermute x4, starting transfers between devices: 9.18 us -> 7.68 us  [the longest x1 4.8 us: program(): own_halo = lax.ppermute(straight_rows, ('ang', 'row'), straight)]
    pallas_call x0 -> x1, Pallas kernels: none -> 1.31 us  [pack(): pl.pallas_call(pack_kernel, name='pack', out_shape=(image(CH + 1, SLAB),...]
  transfers between devices with their start and end apart: 4 -> 4, of which waited for: 0 -> 1; matrix products, arithmetic and copies ran while one was open for 5% -> 0% of each run, Pallas kernels for 24% -> 18%
where the time goes in v2:
time: 72.8 us; the launch traced here: 71.5 us
  blocking collectives  26.3 us (36%)
  Pallas kernels  24 us (33%)
  waiting for transfers between devices  12.8 us (18%)
  starting transfers between devices  7.68 us (11%)
  between operations  0.73 us (1%)
    all_to_all x1, blocking collectives, program(): lax.all_to_all(grads.reshape(HALF, 8, COLS), 'ang', 0, 0, axis_index_grou...  26.3 us
    pallas_call x2, Pallas kernels, track(): pl.pallas_call(kernel, name='track', out_shape=jax.ShapeDtypeStruct((8 *...  18.1 us
    ppermute x1, waiting for transfers between devices, program(): own_halo = lax.ppermute(straight_rows, ('ang', 'row'), straight)  12.8 us
    ppermute x1, starting transfers between devices, program(): own_halo = lax.ppermute(straight_rows, ('ang', 'row'), straight)  4.8 us
    pallas_call x1, Pallas kernels, prepare(): pl.pallas_call(prepare_kernel, name='prepare', out_shape=(jax.ShapeDtypeS...  3.62 us
    ppermute x1, starting transfers between devices, program(): got_0 = lax.ppermute(send_0, 'ang', route)  2.12 us
  transfers between devices with their start and end apart: 4, of which 1 were waited for; matrix products, arithmetic and copies ran while one was open for 0% of the time, Pallas kernels for 18%

profile of v2, /device:TPU:1, one launch (start us, length us, event | category | flops | bytes accessed | tf_op | source)
XLA Modules:
  0.0 71.5 jit_solution(15102709454364113982)
XLA Ops:
  0.7 1.3 %pack.1 = (bf16[21,72,128]{2,1,0:T(8,128)(2,1)S(1)}, bf16[21,72,128]{2,1,0:T(8,128)(2,1)S(1)}, bf16[3,20,8,128]{3,2,1,0:T(8,128)(2,1)S(1)}, bf16[2,20,8,128]{3,2,1,0:T(8,128)(2,1)S(1)}) custom-call(s32[1]{0:T(128)} %bitcast.1.code.refs_0_, bf16[2,20,128,128]{3,2,1,0:T(8,128)(2,1)} %sample.3, bf16[20,128,128]{2,1,0:T(8,128)(2,1)} %flat_all.1, ...), custom_call_target="tpu_custom_call" | custom-call | tf_op jit(solution)/shard_map/pack/pallas_call | solution.py:62
  2.0 2.1 %collective-permute-start.3 = (bf16[21,72,128]{2,1,0:T(8,128)(2,1)S(1)}, bf16[21,72,128]{2,1,0:T(8,128)(2,1)S(1)}, u32[]{:S(2)}, u32[]{:S(2)}) collective-permute-start(bf16[21,72,128]{2,1,0:T(8,128)(2,1)S(1)} %get-tuple-element.28), channel_id=1, source_target_pairs={{0,128},{2,130},{4,132},{6,134},{8,136},{10,138},{12,140},{14,142}... | collective-permute-start | bytes 1161224 | tf_op jit(solution)/shard_map/ppermute | solution.py:403
  4.1 0.1 collective-permute-start.1
  4.2 4.8 %collective-permute-start = (bf16[3,20,8,128]{3,2,1,0:T(8,128)(2,1)S(1)}, bf16[3,20,8,128]{3,2,1,0:T(8,128)(2,1)S(1)}, u32[]{:S(2)}, u32[]{:S(2)}) collective-permute-start(bf16[3,20,8,128]{3,2,1,0:T(8,128)(2,1)S(1)} %get-tuple-element.17), channel_id=1, source_target_pairs={{0,1},{2,3},{4,5},{6,7},{8,9},{10,11},{12,13},{14,15},{16,17},{18,... | collective-permute-start | bytes 368648 | tf_op jit(solution)/shard_map/ppermute | solution.py:402
  9.0 0.7 collective-permute-start.2
  9.7 12.8 %collective-permute-done.halo.refs_4_.own_halo = bf16[3,20,8,128]{3,2,1,0:T(8,128)(2,1)S(1)} collective-permute-done((bf16[3,20,8,128]{3,2,1,0:T(8,128)(2,1)S(1)}, bf16[3,20,8,128]{3,2,1,0:T(8,128)(2,1)S(1)}, u32[]{:S(2)}, u32[]{:S(2)}) %collective-permute-start) | collective-permute-done | bytes 122912 | tf_op jit(solution)/shard_map/ppermute | solution.py:402
  22.5 3.6 %prepare.1 = (f32[7,20,80,128]{3,2,1,0:T(8,128)S(1)}, f32[7,88,128]{2,1,0:T(8,128)S(1)}, bf16[2,20,72,128]{3,2,1,0:T(8,128)(2,1)S(1)}, s32[2,2,64,128]{3,2,1,0:T...) custom-call(s32[1]{0:T(128)} %bitcast.1.code.refs_0_, ...), custom_call_target="tpu_custom_call" | custom-call | tf_op jit(solution)/shard_map/prepare/pallas_call | solution.py:159
  26.1 0.0 collective-permute-done.2.refs_5_.got_halo
  26.1 0.0 collective-permute-done.3.refs_3_
  26.1 9.1 %track.2.before = f32[512,128]{1,0:T(8,128)S(1)} custom-call(s32[1]{0:T(128)} %bitcast.1.code.refs_0_, bf16[2,20,72,128]{3,2,1,0:T(8,128)(2,1)S(1)} %get-tuple-element.18.refs_1_.own, s32[2,2,64,128]{3,2,1,0:T(8,128)S(1)} %get-tuple-element.19.refs_2_.own_peaks, bf16[21,72,128]{2,1,0:T(8,128)(2,1)S(1)} %collective-permute-done.3.refs_3_, ...), custom_call_target="tpu_custom_call" | custom-call | tf_op jit(solution)/shard_map/track/pallas_call | solution.py:329
  35.2 0.0 collective-permute-done.1.got
  35.2 9.1 %track.3 = f32[512,128]{1,0:T(8,128)S(1)} custom-call(s32[1]{0:T(128)} %bitcast.1.code.refs_0_, bf16[2,20,72,128]{3,2,1,0:T(8,128)(2,1)S(1)} %get-tuple-element.18.refs_1_.own, s32[2,2,64,128]{3,2,1,0:T(8,128)S(1)} %get-tuple-element.19.refs_2_.own_peaks, bf16[21,72,128]{2,1,0:T(8,128)(2,1)S(1)} %collective-permute-done.1.got, ...), custom_call_target="tpu_custom_call" | custom-call | tf_op jit(solution)/shard_map/track/pallas_call | solution.py:329
  44.3 26.3 %all_to_all.5 = f32[64,8,128]{2,1,0:T(8,128)S(1)} all-to-all(f32[64,8,128]{2,1,0:T(8,128)S(1)} %bitcast.8), channel_id=1, replica_groups={{0,2,4,6,8,10,12,14,16,18,20,22,24,26,28,30,32,34,36,38,40,42,44,46,48,..., dimensions={0} | all-to-all | bytes 524288 | tf_op jit(solution)/shard_map/all_to_all | solution.py:414
  70.6 0.9 %finish.1 = f32[2,256,128]{2,1,0:T(8,128)} custom-call(f32[512,128]{1,0:T(8,128)S(1)} %bitcast.9), custom_call_target="tpu_custom_call" | custom-call | tf_op jit(solution)/shard_map/finish/pallas_call | solution.py:378
Async XLA Ops:
  2.0 24.1 %collective-permute-start.3 = (bf16[21,72,128]{2,1,0:T(8,128)(2,1)S(1)}, bf16[21,72,128]{2,1,0:T(8,128)(2,1)S(1)}, u32[]{:S(2)}, u32[]{:S(2)}) collective-permute-start(bf16[21,72,128]{2,1,0:T(8,128)(2,1)S(1)} %get-tuple-element.28), channel_id=1, source_target_pairs={{0,128},{2,130},{4,132},{6,134},{8,136},{10,138},{12,140},{14,142}... | collective-permute-start | bytes 1161224 | tf_op jit(solution)/shard_map/ppermute | solution.py:403
  4.1 31.1 %collective-permute-start.1 = (bf16[21,72,128]{2,1,0:T(8,128)(2,1)S(1)}, bf16[21,72,128]{2,1,0:T(8,128)(2,1)S(1)}, u32[]{:S(2)}, u32[]{:S(2)}) collective-permute-start(bf16[21,72,128]{2,1,0:T(8,128)(2,1)S(1)} %get-tuple-element.20), channel_id=1, source_target_pairs={{0,128},{2,130},{4,132},{6,134},{8,136},{10,138},{12,140},{14,142}... | collective-permute-start | bytes 1161224 | tf_op jit(solution)/shard_map/ppermute | solution.py:405
  4.2 18.3 %collective-permute-start = (bf16[3,20,8,128]{3,2,1,0:T(8,128)(2,1)S(1)}, bf16[3,20,8,128]{3,2,1,0:T(8,128)(2,1)S(1)}, u32[]{:S(2)}, u32[]{:S(2)}) collective-permute-start(bf16[3,20,8,128]{3,2,1,0:T(8,128)(2,1)S(1)} %get-tuple-element.17), channel_id=1, source_target_pairs={{0,1},{2,3},{4,5},{6,7},{8,9},{10,11},{12,13},{14,15},{16,17},{18,... | collective-permute-start | bytes 368648 | tf_op jit(solution)/shard_map/ppermute | solution.py:402
  9.0 17.1 %collective-permute-start.2 = (bf16[2,20,8,128]{3,2,1,0:T(8,128)(2,1)S(1)}, bf16[2,20,8,128]{3,2,1,0:T(8,128)(2,1)S(1)}, u32[]{:S(2)}, u32[]{:S(2)}) collective-permute-start(bf16[2,20,8,128]{3,2,1,0:T(8,128)(2,1)S(1)} %get-tuple-element.21), channel_id=1, source_target_pairs={{128,1},{130,3},{132,5},{134,7},{136,9},{138,11},{140,13},{142,15}... | collective-permute-start | bytes 245768 | tf_op jit(solution)/shard_map/ppermute | solution.py:404
